TPU v7x, 32 devices: a whole 2x2x4 slice. The times are simulated.
32 devices in a mesh: groups: 2 (over x), tiles: 16 (over z, y, core).
Axes of the slice: x: 2, y: 2, z: 4, core: 2. Of those that a mesh axis runs over, the one named last changes fastest.
Arguments:
- pieces: bfloat16 [512, 6, 128, 128], P(('groups', 'tiles')), parts along dimension 0, may hold values from -6 to 6
- piece_blend: int32 [512], P(('groups', 'tiles')), parts along dimension 0, may hold values from 0 to 63, as said below
- corners: int32 [512, 2], P(('groups', 'tiles')), parts along dimension 0, may hold values from -96 to 223
- blend_home: int32 [128], P('groups'), parts along dimension 0, may hold values from 0 to 63, as said below
- source_count: int32 [128], P(('groups', 'tiles')), parts along dimension 0, may hold values from 1 to 4
- footprint: int32 [128, 128, 128], P(('groups', 'tiles')), parts along dimension 0, may hold values from 0 to 4
- spectra: float32 [128, 4, 6], P(('groups', 'tiles')), parts along dimension 0, may hold values from 0.2 to 1
- giant_pieces: bfloat16 [32, 6, 128, 128], P(('groups', 'tiles')), parts along dimension 0, may hold values from -6 to 6
- giant_footprint: int32 [32, 128, 128], P(('groups', 'tiles')), parts along dimension 0, may hold values from 0 to 4
- giant_spectra: float32 [32, 4, 6], P(('groups', 'tiles')), parts along dimension 0, may hold values from 0.2 to 1
- psf_matrix: bfloat16 [6, 128, 128], replicated, may hold values from 0 to 1
Outputs:
- blend_morph: bfloat16 [128, 4, 128, 128], P(('groups', 'tiles')), parts along dimension 0
- blend_spectra: bfloat16 [128, 4, 6], P(('groups', 'tiles')), parts along dimension 0
- tile_model: float32 [32, 6, 256, 256], P(('groups', 'tiles')), parts along dimension 0
- giant_morph: float32 [32, 4, 128, 128], P(('groups', 'tiles')), parts along dimension 0
There are 2 independent parts, one for each index of `groups`. A program takes and returns all parts, laid end to end along the dimension named above; an argument that names none is the same for every part. Nothing has to cross between parts.
Inputs may be any that keep to these rules, and one draw needn't show every extreme that they name: `piece_blend`: at most 2 pieces of one device belong to blends of one owner; in every draw some owner gets exactly 2 pieces from every device. `blend_home`: A permutation of 0 to 63.
All inputs are finite; a program needn't handle non-finite values.
Results may differ from a plain program's by a relative error of at most 0.006.
Values may be sent and summed in bfloat16 or wider, within the bound.
A program may use at most 128 MiB of HBM per device.

v0:
```python
import jax
import jax.numpy as jnp
from jax import lax
from jax.sharding import PartitionSpec as P

SLOT_CAP = 2
TILE = 256
ITERS = 3


step_size = 0.1


def swapped(block, axis, bit):
    count = lax.axis_size(axis)
    route = []
    for low in range(count):
        high = low | 1 << bit
        if high != low and high < count:
            route += [(low, high), (high, low)]
    return lax.ppermute(block, axis, route)


def psf_blur(mix, psf_matrix):
    half_way = jnp.einsum(
        "bij,nbjk->nbik", psf_matrix, mix, preferred_element_type=jnp.float32
    ).astype(jnp.bfloat16)
    return jnp.einsum("nbij,bkj->nbik", half_way, psf_matrix, preferred_element_type=jnp.float32)


def adjoint(resid, psf_matrix):
    half_way = jnp.einsum(
        "bji,nbjk->nbik", psf_matrix, resid, preferred_element_type=jnp.float32
    ).astype(jnp.bfloat16)
    return jnp.einsum("nbij,bjk->nbik", half_way, psf_matrix, preferred_element_type=jnp.float32)


def combine(sed, morph):
    return jnp.einsum("nkb,nkij->nbij", sed, morph, precision=lax.Precision.HIGHEST)


def initial(image, labels, active):
    source_total = active.shape[1]
    base_map = jnp.maximum(jnp.mean(image, axis=1), 0.0)
    marks = (
        labels[:, None] == (jnp.arange(source_total, dtype=jnp.int32) + 1)[None, :, None, None]
    ).astype(jnp.float32)
    return marks * base_map[:, None] * active[:, :, None, None]


def refine(image, morph, sed, active, psf_matrix, total):
    for iteration in range(ITERS):
        model_now = total(psf_blur(combine(sed, morph).astype(jnp.bfloat16), psf_matrix))
        resid = (image - model_now).astype(jnp.bfloat16)
        grad = adjoint(resid, psf_matrix)
        inner = jnp.einsum("nkij,nbij->nkb", morph, grad, precision=lax.Precision.HIGHEST)
        energy = jnp.sum(morph * morph, axis=(2, 3))
        push = jnp.einsum("nkb,nbij->nkij", sed, grad, precision=lax.Precision.HIGHEST)
        sed_next = jnp.maximum(sed + inner / (energy + 1.0)[:, :, None], 0.0) * active[:, :, None]
        morph = jnp.maximum(morph + step_size * push, 0.0) * active[:, :, None, None]
        sed = sed_next
    return (morph, sed)


def group_total(field_sum):
    for bit_number in range(3):
        field_sum = field_sum + swapped(field_sum.astype(jnp.bfloat16), "tiles", bit_number).astype(
            field_sum.dtype
        )
    return field_sum


def on_device(
    pieces,
    piece_blend,
    corners,
    blend_home,
    source_count,
    footprint,
    spectra,
    giant_pieces,
    giant_footprint,
    giant_spectra,
    psf_matrix,
):
    tile_count = lax.axis_size("tiles")
    my_index = lax.axis_index("tiles")
    piece_count = pieces.shape[0]
    band_count = pieces.shape[1]
    patch_side = pieces.shape[2]
    owned_count = footprint.shape[0]
    blend_count = blend_home.shape[0]
    source_total = spectra.shape[1]
    lookup = piece_blend[:, None] == jnp.arange(blend_count, dtype=jnp.int32)[None, :]
    piece_home = jnp.sum(jnp.where(lookup, blend_home[None, :], 0), axis=1)
    every_home = lax.all_gather(piece_home, "tiles", axis=0, tiled=True).reshape(
        tile_count, piece_count
    )
    owners = every_home // owned_count
    places = every_home % owned_count
    earlier = jnp.arange(piece_count)[None, :] < jnp.arange(piece_count)[:, None]
    same_owner = owners[:, :, None] == owners[:, None, :]
    piece_rank = jnp.sum(same_owner & earlier[None], axis=2)
    send_row = owners * SLOT_CAP + piece_rank
    my_rows = lax.dynamic_index_in_dim(send_row, my_index, 0, keepdims=False)
    row_count = tile_count * SLOT_CAP
    selector = (my_rows[None, :] == jnp.arange(row_count)[:, None]).astype(jnp.bfloat16)
    outgoing = jnp.einsum(
        "rp,pbij->rbij", selector, pieces, preferred_element_type=jnp.float32
    ).astype(jnp.bfloat16)
    incoming = lax.all_to_all(
        outgoing.reshape(tile_count, SLOT_CAP, band_count, patch_side, patch_side),
        "tiles",
        split_axis=0,
        concat_axis=0,
        tiled=True,
    )
    target_rows = my_index * SLOT_CAP + jnp.arange(SLOT_CAP)
    matched = send_row[:, None, :] == target_rows[None, :, None]
    blend_slot = jnp.sum(jnp.where(matched, places[:, None, :], 0), axis=2)
    is_live = jnp.any(matched, axis=2)
    assignment = (blend_slot[:, :, None] == jnp.arange(owned_count)[None, None, :]) & is_live[
        :, :, None
    ]
    assignment = assignment.reshape(row_count, owned_count).astype(jnp.bfloat16)
    blend_image = jnp.einsum(
        "rq,rbij->qbij",
        assignment,
        incoming.reshape(row_count, band_count, patch_side, patch_side),
        preferred_element_type=jnp.float32,
    )
    active = (jnp.arange(source_total, dtype=jnp.int32)[None, :] < source_count[:, None]).astype(
        jnp.float32
    )
    morph = initial(blend_image, footprint, active)
    sed = spectra * active[:, :, None]
    morph, sed = refine(blend_image, morph, sed, active, psf_matrix, lambda summed: summed)
    final_morph = morph.astype(jnp.bfloat16)
    final_sed = sed.astype(jnp.bfloat16)
    blend_mix = combine(final_sed.astype(jnp.float32), final_morph.astype(jnp.float32)).astype(
        jnp.bfloat16
    )
    blend_model = psf_blur(blend_mix, psf_matrix).astype(jnp.bfloat16)
    back_model = jnp.einsum(
        "rq,qbij->rbij", assignment, blend_model, preferred_element_type=jnp.float32
    ).astype(jnp.bfloat16)
    got_model = lax.all_to_all(
        back_model.reshape(tile_count, SLOT_CAP, band_count, patch_side, patch_side),
        "tiles",
        split_axis=0,
        concat_axis=0,
        tiled=True,
    )
    piece_model = jnp.einsum(
        "rp,rbij->pbij",
        selector,
        got_model.reshape(row_count, band_count, patch_side, patch_side),
        preferred_element_type=jnp.float32,
    ).astype(jnp.bfloat16)
    margin = patch_side - patch_side // 4
    canvas_start = jnp.zeros((band_count, TILE + 2 * margin, TILE + 2 * margin), jnp.float32)

    def place(piece_index, canvas):
        patch_model = lax.dynamic_index_in_dim(piece_model, piece_index, 0, keepdims=False).astype(
            jnp.float32
        )
        row_start = corners[piece_index, 0] + margin
        col_start = corners[piece_index, 1] + margin
        anchor = (jnp.zeros((), jnp.int32), row_start, col_start)
        region = lax.dynamic_slice(canvas, anchor, (band_count, patch_side, patch_side))
        return lax.dynamic_update_slice(canvas, region + patch_model, anchor)

    canvas = lax.fori_loop(0, piece_count, place, canvas_start)
    tile_model = canvas[None, :, margin : margin + TILE, margin : margin + TILE]
    giant_image = group_total(giant_pieces.astype(jnp.float32))
    giant_active = jnp.ones((1, giant_spectra.shape[1]), jnp.float32)
    giant_start = initial(giant_image, giant_footprint, giant_active)
    giant_morph, giant_sed = refine(
        giant_image, giant_start, giant_spectra, giant_active, psf_matrix, group_total
    )
    return (final_morph, final_sed, tile_model, giant_morph)


def solution(mesh):
    in_specs = (
        P(("groups", "tiles"), None, None, None),
        P(("groups", "tiles")),
        P(("groups", "tiles"), None),
        P("groups"),
        P(("groups", "tiles")),
        P(("groups", "tiles"), None, None),
        P(("groups", "tiles"), None, None),
        P(("groups", "tiles"), None, None, None),
        P(("groups", "tiles"), None, None),
        P(("groups", "tiles"), None, None),
        P(),
    )
    out_specs = (
        P(("groups", "tiles"), None, None, None),
        P(("groups", "tiles"), None, None),
        P(("groups", "tiles"), None, None, None),
        P(("groups", "tiles"), None, None, None),
    )
    return jax.shard_map(
        on_device, mesh=mesh, in_specs=in_specs, out_specs=out_specs, check_vma=False
    )
```

profile of v0, /device:TPU:26, one launch (start us, length us, event | category | flops | bytes accessed | tf_op | source)
XLA Modules:
  0.0 640.5 jit_solution(16896176282940361676)
XLA Ops:
  3.8 8.9 %all-reduce = s32[256]{0:T(256)S(1)} all-reduce(s32[256]{0:T(256)S(1)} %dynamic-update-slice), channel_id=1, replica_groups=mesh['groups'=2,'tiles'=16] {'tiles'}, use_global_device_ids=true, to_apply=%add | all-reduce | flops 256 | bytes 2048
  13.3 2.5 convolution_convert_fusion.1
  15.8 5.4 copy.230
  21.2 8.4 %all-to-all-start = ((bf16[16,2,6,128,128]{4,1,3,2,0:T(2,128)(2,1)}), bf16[16,2,6,128,128]{4,1,3,2,0:T(2,128)(2,1)}, u32[]{:S(2)}, u32[]{:S(2)}) async-start(bf16[16,2,6,128,128]{4,1,3,2,0:T(2,128)(2,1)} %copy.230), calls=%async_computation | async-start | bytes 12582912 | tf_op jit(solution)/shard_map/all_to_all | solution.py:111
  30.5 126.6 %all-to-all-done = bf16[16,2,6,128,128]{4,1,3,2,0:T(2,128)(2,1)} async-done(((bf16[16,2,6,128,128]{4,1,3,2,0:T(2,128)(2,1)}), bf16[16,2,6,128,128]{4,1,3,2,0:T(2,128)(2,1)}, u32[]{:S(2)}, u32[]{:S(2)}) %all-to-all-start) | async-done | bytes 6291488 | tf_op jit(solution)/shard_map/all_to_all | solution.py:111
  157.1 6.8 %bitcast_reduce_fusion = (f32[4,128,128]{2,0,1:T(4,128)S(1)}, f32[4,6,128,128,1]{3,0,4,2,1:T(4,128)S(1)}) fusion(bf16[16,2,6,128,128]{4,1,3,2,0:T(2,128)(2,1)} %all-to-all-done, s32[16,2]{0,1:T(2,128)S(1)} %fusion.219, pred[16,2]{0,1:T(4,128)(4,1)S(1)} %compare_reduce_fusion), kind=kOutput, calls=%fused_computation.27 | convolution fusion | flops 25493760 | bytes 8126624 | tf_op jit(solution)/shard_map/rq,rbij->qbij/dot_general | solution.py:126
  164.5 2.5 convolution_convert_fusion.6
  167.0 1.8 fusion.67
  168.8 2.6 fusion.17
  171.5 1.8 convolution_bitcast_fusion.2
  173.3 5.3 multiply_reduce_fusion.1
  178.6 5.7 fusion.132
  184.3 3.3 convolution_convert_fusion.5
  187.6 3.0 fusion.66
  190.6 2.6 fusion.16
  193.2 1.8 convolution_bitcast_fusion.1
  195.0 5.2 multiply_reduce_fusion
  200.2 5.4 fusion.120
  205.7 3.2 convolution_convert_fusion.4
  208.9 3.0 fusion.65
  211.9 3.5 fusion.15
  215.4 1.8 convolution_bitcast_fusion
  217.2 3.2 fusion.54
  220.4 5.3 fusion.108
  227.0 2.1 convolution_convert_fusion
  229.1 5.4 copy.259
  234.5 15.0 %all-to-all-start.1 = ((bf16[16,2,6,128,128]{4,1,3,2,0:T(2,128)(2,1)}), bf16[16,2,6,128,128]{4,1,3,2,0:T(2,128)(2,1)}, u32[]{:S(2)}, u32[]{:S(2)}) async-start(bf16[16,2,6,128,128]{4,1,3,2,0:T(2,128)(2,1)} %copy.259), calls=%async_computation.1 | async-start | bytes 12582912 | tf_op jit(solution)/shard_map/all_to_all | solution.py:147
  249.7 1.6 collective-permute-done
  251.3 1.5 collective-permute-start.1
  252.9 37.6 %collective-permute-done.1 = bf16[1,6,128,128]{3,2,1,0:T(8,128)(2,1)S(1)} collective-permute-done((bf16[1,6,128,128]{3,2,1,0:T(8,128)(2,1)S(1)}, bf16[1,6,128,128]{3,2,1,0:T(8,128)(2,1)S(1)}, u32[]{:S(2)}, u32[]{:S(2)}) %collective-permute-start.1) | collective-permute-done | bytes 196640 | tf_op jit(solution)/shard_map/ppermute | solution.py:21
  290.7 65.0 %collective-permute-done.2 = bf16[1,6,128,128]{3,2,1,0:T(8,128)(2,1)S(1)} collective-permute-done((bf16[1,6,128,128]{3,2,1,0:T(8,128)(2,1)S(1)}, bf16[1,6,128,128]{3,2,1,0:T(8,128)(2,1)S(1)}, u32[]{:S(2)}, u32[]{:S(2)}) %collective-permute-start.2) | collective-permute-done | bytes 196640 | tf_op jit(solution)/shard_map/ppermute | solution.py:21
  357.1 1.4 collective-permute-done.3
  358.6 1.6 collective-permute-start.4
  360.4 13.4 %collective-permute-done.4 = bf16[1,6,128,128]{3,2,1,0:T(8,128)(2,1)S(1)} collective-permute-done((bf16[1,6,128,128]{3,2,1,0:T(8,128)(2,1)S(1)}, bf16[1,6,128,128]{3,2,1,0:T(8,128)(2,1)S(1)}, u32[]{:S(2)}, u32[]{:S(2)}) %collective-permute-start.4) | collective-permute-done | bytes 196640 | tf_op jit(solution)/shard_map/ppermute | solution.py:21
  374.0 16.3 %collective-permute-done.5 = bf16[1,6,128,128]{3,2,1,0:T(8,128)(2,1)S(1)} collective-permute-done((bf16[1,6,128,128]{3,2,1,0:T(8,128)(2,1)S(1)}, bf16[1,6,128,128]{3,2,1,0:T(8,128)(2,1)S(1)}, u32[]{:S(2)}, u32[]{:S(2)}) %collective-permute-start.5) | collective-permute-done | bytes 196640 | tf_op jit(solution)/shard_map/ppermute | solution.py:21
  391.8 1.5 fusion.90
  394.6 1.4 collective-permute-done.6
  396.2 6.9 %collective-permute-done.7 = bf16[1,6,128,128]{3,2,1,0:T(8,128)(2,1)S(1)} collective-permute-done((bf16[1,6,128,128]{3,2,1,0:T(8,128)(2,1)S(1)}, bf16[1,6,128,128]{3,2,1,0:T(8,128)(2,1)S(1)}, u32[]{:S(2)}, u32[]{:S(2)}) %collective-permute-start.7) | collective-permute-done | bytes 196640 | tf_op jit(solution)/shard_map/ppermute | solution.py:21
  403.3 6.1 collective-permute-done.8
  410.7 1.5 fusion.95
  413.5 1.4 collective-permute-done.9
  415.6 6.4 collective-permute-done.10
  422.5 5.8 collective-permute-done.11
  431.2 6.0 copy.260
  438.2 2.5 copy.261
  440.7 3.1 broadcast_in_dim.32
  443.9 192.7 %while.16 = (s32[]{:T(128)}, f32[6,448,448]{2,1,0:T(8,128)}, s32[16,2]{0,1:T(2,128)S(1)}, bf16[16,6,128,128]{3,2,1,0:T(8,128)(2,1)}, s32[]{:T(128)}, /*index=5*/s32[1,1]{0,1:T(1,128)}, s32[]{:T(128)}, s32[1,1]{0,1:T(1,128)}) while((s32[]{:T(128)}, f32[6,448,448]{2,1,0:T(8,128)}, s32[16,2]{0,1:T(2,128)S(1)}, ...), condition=%wide.region_9.10_spmd, body=%wide.region_8.9_spmd.sunk | while | flops 196618 | bytes 1769685 | solution.py:173
  448.2 7.7 %dynamic_update_slice.12 = f32[6,448,448]{2,1,0:T(8,128)} dynamic-update-slice(f32[6,448,448]{2,1,0:T(8,128)} %get-tuple-element.243, f32[6,128,128]{2,1,0:T(8,128)S(1)} %convert_add_fusion.18, s32[]{:T(128)} %constant.120.clone.1..sunk, s32[]{:T(128)S(6)} %select_n.90, s32[]{:T(128)S(6)} %select_n.91) | dynamic-update-slice | bytes 786436 | tf_op jit(solution)/shard_map/while/body/eval_jaxpr/dynamic_update_slice | solution.py:171
  460.3 7.7 %dynamic_update_slice.12 = f32[6,448,448]{2,1,0:T(8,128)} dynamic-update-slice(f32[6,448,448]{2,1,0:T(8,128)} %get-tuple-element.243, f32[6,128,128]{2,1,0:T(8,128)S(1)} %convert_add_fusion.18, s32[]{:T(128)} %constant.120.clone.1..sunk, s32[]{:T(128)S(6)} %select_n.90, s32[]{:T(128)S(6)} %select_n.91) | dynamic-update-slice | bytes 786436 | tf_op jit(solution)/shard_map/while/body/eval_jaxpr/dynamic_update_slice | solution.py:171
  472.4 7.7 %dynamic_update_slice.12 = f32[6,448,448]{2,1,0:T(8,128)} dynamic-update-slice(f32[6,448,448]{2,1,0:T(8,128)} %get-tuple-element.243, f32[6,128,128]{2,1,0:T(8,128)S(1)} %convert_add_fusion.18, s32[]{:T(128)} %constant.120.clone.1..sunk, s32[]{:T(128)S(6)} %select_n.90, s32[]{:T(128)S(6)} %select_n.91) | dynamic-update-slice | bytes 786436 | tf_op jit(solution)/shard_map/while/body/eval_jaxpr/dynamic_update_slice | solution.py:171
  484.5 7.7 %dynamic_update_slice.12 = f32[6,448,448]{2,1,0:T(8,128)} dynamic-update-slice(f32[6,448,448]{2,1,0:T(8,128)} %get-tuple-element.243, f32[6,128,128]{2,1,0:T(8,128)S(1)} %convert_add_fusion.18, s32[]{:T(128)} %constant.120.clone.1..sunk, s32[]{:T(128)S(6)} %select_n.90, s32[]{:T(128)S(6)} %select_n.91) | dynamic-update-slice | bytes 786436 | tf_op jit(solution)/shard_map/while/body/eval_jaxpr/dynamic_update_slice | solution.py:171
  496.6 7.6 %dynamic_update_slice.12 = f32[6,448,448]{2,1,0:T(8,128)} dynamic-update-slice(f32[6,448,448]{2,1,0:T(8,128)} %get-tuple-element.243, f32[6,128,128]{2,1,0:T(8,128)S(1)} %convert_add_fusion.18, s32[]{:T(128)} %constant.120.clone.1..sunk, s32[]{:T(128)S(6)} %select_n.90, s32[]{:T(128)S(6)} %select_n.91) | dynamic-update-slice | bytes 786436 | tf_op jit(solution)/shard_map/while/body/eval_jaxpr/dynamic_update_slice | solution.py:171
  508.6 7.7 %dynamic_update_slice.12 = f32[6,448,448]{2,1,0:T(8,128)} dynamic-update-slice(f32[6,448,448]{2,1,0:T(8,128)} %get-tuple-element.243, f32[6,128,128]{2,1,0:T(8,128)S(1)} %convert_add_fusion.18, s32[]{:T(128)} %constant.120.clone.1..sunk, s32[]{:T(128)S(6)} %select_n.90, s32[]{:T(128)S(6)} %select_n.91) | dynamic-update-slice | bytes 786436 | tf_op jit(solution)/shard_map/while/body/eval_jaxpr/dynamic_update_slice | solution.py:171
  520.7 7.7 %dynamic_update_slice.12 = f32[6,448,448]{2,1,0:T(8,128)} dynamic-update-slice(f32[6,448,448]{2,1,0:T(8,128)} %get-tuple-element.243, f32[6,128,128]{2,1,0:T(8,128)S(1)} %convert_add_fusion.18, s32[]{:T(128)} %constant.120.clone.1..sunk, s32[]{:T(128)S(6)} %select_n.90, s32[]{:T(128)S(6)} %select_n.91) | dynamic-update-slice | bytes 786436 | tf_op jit(solution)/shard_map/while/body/eval_jaxpr/dynamic_update_slice | solution.py:171
  532.8 7.7 %dynamic_update_slice.12 = f32[6,448,448]{2,1,0:T(8,128)} dynamic-update-slice(f32[6,448,448]{2,1,0:T(8,128)} %get-tuple-element.243, f32[6,128,128]{2,1,0:T(8,128)S(1)} %convert_add_fusion.18, s32[]{:T(128)} %constant.120.clone.1..sunk, s32[]{:T(128)S(6)} %select_n.90, s32[]{:T(128)S(6)} %select_n.91) | dynamic-update-slice | bytes 786436 | tf_op jit(solution)/shard_map/while/body/eval_jaxpr/dynamic_update_slice | solution.py:171
  544.9 7.4 %dynamic_update_slice.12 = f32[6,448,448]{2,1,0:T(8,128)} dynamic-update-slice(f32[6,448,448]{2,1,0:T(8,128)} %get-tuple-element.243, f32[6,128,128]{2,1,0:T(8,128)S(1)} %convert_add_fusion.18, s32[]{:T(128)} %constant.120.clone.1..sunk, s32[]{:T(128)S(6)} %select_n.90, s32[]{:T(128)S(6)} %select_n.91) | dynamic-update-slice | bytes 786436 | tf_op jit(solution)/shard_map/while/body/eval_jaxpr/dynamic_update_slice | solution.py:171
  556.7 7.7 %dynamic_update_slice.12 = f32[6,448,448]{2,1,0:T(8,128)} dynamic-update-slice(f32[6,448,448]{2,1,0:T(8,128)} %get-tuple-element.243, f32[6,128,128]{2,1,0:T(8,128)S(1)} %convert_add_fusion.18, s32[]{:T(128)} %constant.120.clone.1..sunk, s32[]{:T(128)S(6)} %select_n.90, s32[]{:T(128)S(6)} %select_n.91) | dynamic-update-slice | bytes 786436 | tf_op jit(solution)/shard_map/while/body/eval_jaxpr/dynamic_update_slice | solution.py:171
  568.8 7.7 %dynamic_update_slice.12 = f32[6,448,448]{2,1,0:T(8,128)} dynamic-update-slice(f32[6,448,448]{2,1,0:T(8,128)} %get-tuple-element.243, f32[6,128,128]{2,1,0:T(8,128)S(1)} %convert_add_fusion.18, s32[]{:T(128)} %constant.120.clone.1..sunk, s32[]{:T(128)S(6)} %select_n.90, s32[]{:T(128)S(6)} %select_n.91) | dynamic-update-slice | bytes 786436 | tf_op jit(solution)/shard_map/while/body/eval_jaxpr/dynamic_update_slice | solution.py:171
  580.8 7.7 %dynamic_update_slice.12 = f32[6,448,448]{2,1,0:T(8,128)} dynamic-update-slice(f32[6,448,448]{2,1,0:T(8,128)} %get-tuple-element.243, f32[6,128,128]{2,1,0:T(8,128)S(1)} %convert_add_fusion.18, s32[]{:T(128)} %constant.120.clone.1..sunk, s32[]{:T(128)S(6)} %select_n.90, s32[]{:T(128)S(6)} %select_n.91) | dynamic-update-slice | bytes 786436 | tf_op jit(solution)/shard_map/while/body/eval_jaxpr/dynamic_update_slice | solution.py:171
  592.9 7.7 %dynamic_update_slice.12 = f32[6,448,448]{2,1,0:T(8,128)} dynamic-update-slice(f32[6,448,448]{2,1,0:T(8,128)} %get-tuple-element.243, f32[6,128,128]{2,1,0:T(8,128)S(1)} %convert_add_fusion.18, s32[]{:T(128)} %constant.120.clone.1..sunk, s32[]{:T(128)S(6)} %select_n.90, s32[]{:T(128)S(6)} %select_n.91) | dynamic-update-slice | bytes 786436 | tf_op jit(solution)/shard_map/while/body/eval_jaxpr/dynamic_update_slice | solution.py:171
  605.0 7.7 %dynamic_update_slice.12 = f32[6,448,448]{2,1,0:T(8,128)} dynamic-update-slice(f32[6,448,448]{2,1,0:T(8,128)} %get-tuple-element.243, f32[6,128,128]{2,1,0:T(8,128)S(1)} %convert_add_fusion.18, s32[]{:T(128)} %constant.120.clone.1..sunk, s32[]{:T(128)S(6)} %select_n.90, s32[]{:T(128)S(6)} %select_n.91) | dynamic-update-slice | bytes 786436 | tf_op jit(solution)/shard_map/while/body/eval_jaxpr/dynamic_update_slice | solution.py:171
  617.1 7.4 %dynamic_update_slice.12 = f32[6,448,448]{2,1,0:T(8,128)} dynamic-update-slice(f32[6,448,448]{2,1,0:T(8,128)} %get-tuple-element.243, f32[6,128,128]{2,1,0:T(8,128)S(1)} %convert_add_fusion.18, s32[]{:T(128)} %constant.120.clone.1..sunk, s32[]{:T(128)S(6)} %select_n.90, s32[]{:T(128)S(6)} %select_n.91) | dynamic-update-slice | bytes 786436 | tf_op jit(solution)/shard_map/while/body/eval_jaxpr/dynamic_update_slice | solution.py:171
  628.9 7.7 %dynamic_update_slice.12 = f32[6,448,448]{2,1,0:T(8,128)} dynamic-update-slice(f32[6,448,448]{2,1,0:T(8,128)} %get-tuple-element.243, f32[6,128,128]{2,1,0:T(8,128)S(1)} %convert_add_fusion.18, s32[]{:T(128)} %constant.120.clone.1..sunk, s32[]{:T(128)S(6)} %select_n.90, s32[]{:T(128)S(6)} %select_n.91) | dynamic-update-slice | bytes 786436 | tf_op jit(solution)/shard_map/while/body/eval_jaxpr/dynamic_update_slice | solution.py:171
  636.6 3.5 slice_bitcast_fusion
  (134 shorter events, 51.1 us)
Async XLA Ops:
  0.6 12.7 %copy-start = (bf16[16,6,128,128]{3,2,1,0:T(8,128)(2,1)S(1)}, bf16[16,6,128,128]{3,2,1,0:T(8,128)(2,1)}, u32[]{:S(2)}) copy-start(bf16[16,6,128,128]{3,2,1,0:T(8,128)(2,1)} %param.13) | copy-start | bytes 9437188
  21.2 9.1 %copy-start.15 = (s32[4]{0:T(128)S(1)}, s32[4]{0:T(128)}, u32[]{:S(2)}) copy-start(s32[4]{0:T(128)} %param.17) | copy-start | bytes 52
  21.2 135.9 %all-to-all-start = ((bf16[16,2,6,128,128]{4,1,3,2,0:T(2,128)(2,1)}), bf16[16,2,6,128,128]{4,1,3,2,0:T(2,128)(2,1)}, u32[]{:S(2)}, u32[]{:S(2)}) async-start(bf16[16,2,6,128,128]{4,1,3,2,0:T(2,128)(2,1)} %copy.230), calls=%async_computation | async-start | bytes 12582912 | tf_op jit(solution)/shard_map/all_to_all | solution.py:111
  30.5 133.5 %copy-start.11 = (s32[4,128,128]{2,1,0:T(8,128)S(1)}, s32[4,128,128]{2,1,0:T(8,128)}, u32[]{:S(2)}) copy-start(s32[4,128,128]{2,1,0:T(8,128)} %param.18) | copy-start | bytes 786436
  30.5 134.1 %copy-start.16 = (f32[4,4,6]{2,1,0:T(4,128)S(1)}, f32[4,4,6]{2,1,0:T(4,128)}, u32[]{:S(2)}) copy-start(f32[4,4,6]{2,1,0:T(4,128)} %param.19) | copy-start | bytes 1156
  163.9 3.1 copy-start.2
  173.3 5.3 copy-start.9
  178.6 9.0 %copy-start.4 = (f32[4,4,128,128]{3,1,2,0:T(4,128)}, f32[4,4,128,128]{3,1,2,0:T(4,128)S(1)}, u32[]{:S(2)}) copy-start(f32[4,4,128,128]{3,1,2,0:T(4,128)S(1)} %get-tuple-element.196) | copy-start | bytes 3145732
  195.0 5.2 copy-start.3
  195.0 5.2 copy-start.5
  220.4 5.4 copy-start.6
  225.8 3.3 copy-start.14
  234.5 15.0 %copy-start.8 = (bf16[1,6,128,128]{3,2,1,0:T(8,128)(2,1)S(1)}, bf16[1,6,128,128]{3,2,1,0:T(8,128)(2,1)}, u32[]{:S(2)}) copy-start(bf16[1,6,128,128]{3,2,1,0:T(8,128)(2,1)} %param.20) | copy-start | bytes 589828
  234.5 196.7 %all-to-all-start.1 = ((bf16[16,2,6,128,128]{4,1,3,2,0:T(2,128)(2,1)}), bf16[16,2,6,128,128]{4,1,3,2,0:T(2,128)(2,1)}, u32[]{:S(2)}, u32[]{:S(2)}) async-start(bf16[16,2,6,128,128]{4,1,3,2,0:T(2,128)(2,1)} %copy.259), calls=%async_computation.1 | async-start | bytes 12582912 | tf_op jit(solution)/shard_map/all_to_all | solution.py:147
  249.5 106.2 %copy-start.10 = (s32[1,128,128]{2,1,0:T(8,128)S(1)}, s32[1,128,128]{2,1,0:T(8,128)}, u32[]{:S(2)}) copy-start(s32[1,128,128]{2,1,0:T(8,128)} %param.21) | copy-start | bytes 196612
  249.5 106.3 %copy-start.13 = (f32[1,4,6]{2,1,0:T(4,128)S(1)}, f32[1,4,6]{2,1,0:T(4,128)}, u32[]{:S(2)}) copy-start(f32[1,4,6]{2,1,0:T(4,128)} %param.22) | copy-start | bytes 292
  249.5 1.8 collective-permute-start
  251.3 39.1 %collective-permute-start.1 = (bf16[1,6,128,128]{3,2,1,0:T(8,128)(2,1)S(1)}, bf16[1,6,128,128]{3,2,1,0:T(8,128)(2,1)S(1)}, u32[]{:S(2)}, u32[]{:S(2)}) collective-permute-start(bf16[1,6,128,128]{3,2,1,0:T(8,128)(2,1)S(1)} %fusion.170), channel_id=1, source_target_pairs={{0,2},{2,0},{1,3},{3,1},{4,6},{6,4},{5,7},{7,5},{8,10},{10,8},{9,1... | collective-permute-start | bytes 589832 | tf_op jit(solution)/shard_map/ppermute | solution.py:21
  290.6 65.0 %collective-permute-start.2 = (bf16[1,6,128,128]{3,2,1,0:T(8,128)(2,1)S(1)}, bf16[1,6,128,128]{3,2,1,0:T(8,128)(2,1)S(1)}, u32[]{:S(2)}, u32[]{:S(2)}) collective-permute-start(bf16[1,6,128,128]{3,2,1,0:T(8,128)(2,1)S(1)} %fusion.182), channel_id=1, source_target_pairs={{0,4},{4,0},{1,5},{5,1},{2,6},{6,2},{3,7},{7,3},{8,12},{12,8},{9,1... | collective-permute-start | bytes 589832 | tf_op jit(solution)/shard_map/ppermute | solution.py:21
  357.1 1.5 collective-permute-start.3
  358.6 15.2 %collective-permute-start.4 = (bf16[1,6,128,128]{3,2,1,0:T(8,128)(2,1)S(1)}, bf16[1,6,128,128]{3,2,1,0:T(8,128)(2,1)S(1)}, u32[]{:S(2)}, u32[]{:S(2)}) collective-permute-start(bf16[1,6,128,128]{3,2,1,0:T(8,128)(2,1)S(1)} %fusion.171), channel_id=1, source_target_pairs={{0,2},{2,0},{1,3},{3,1},{4,6},{6,4},{5,7},{7,5},{8,10},{10,8},{9,1... | collective-permute-start | bytes 589832 | tf_op jit(solution)/shard_map/ppermute | solution.py:21
  373.9 16.3 %collective-permute-start.5 = (bf16[1,6,128,128]{3,2,1,0:T(8,128)(2,1)S(1)}, bf16[1,6,128,128]{3,2,1,0:T(8,128)(2,1)S(1)}, u32[]{:S(2)}, u32[]{:S(2)}) collective-permute-start(bf16[1,6,128,128]{3,2,1,0:T(8,128)(2,1)S(1)} %fusion.216), channel_id=1, source_target_pairs={{0,4},{4,0},{1,5},{5,1},{2,6},{6,2},{3,7},{7,3},{8,12},{12,8},{9,1... | collective-permute-start | bytes 589832 | tf_op jit(solution)/shard_map/ppermute | solution.py:21
  394.6 1.5 collective-permute-start.6
  396.1 7.0 %collective-permute-start.7 = (bf16[1,6,128,128]{3,2,1,0:T(8,128)(2,1)S(1)}, bf16[1,6,128,128]{3,2,1,0:T(8,128)(2,1)S(1)}, u32[]{:S(2)}, u32[]{:S(2)}) collective-permute-start(bf16[1,6,128,128]{3,2,1,0:T(8,128)(2,1)S(1)} %fusion.172), channel_id=1, source_target_pairs={{0,2},{2,0},{1,3},{3,1},{4,6},{6,4},{5,7},{7,5},{8,10},{10,8},{9,1... | collective-permute-start | bytes 589832 | tf_op jit(solution)/shard_map/ppermute | solution.py:21
  403.2 6.2 collective-permute-start.8
  413.5 1.5 collective-permute-start.9
  415.0 7.0 %collective-permute-start.10 = (bf16[1,6,128,128]{3,2,1,0:T(8,128)(2,1)S(1)}, bf16[1,6,128,128]{3,2,1,0:T(8,128)(2,1)S(1)}, u32[]{:S(2)}, u32[]{:S(2)}) collective-permute-start(bf16[1,6,128,128]{3,2,1,0:T(8,128)(2,1)S(1)} %fusion.173), channel_id=1, source_target_pairs={{0,2},{2,0},{1,3},{3,1},{4,6},{6,4},{5,7},{7,5},{8,10},{10,8},{9,1... | collective-permute-start | bytes 589832 | tf_op jit(solution)/shard_map/ppermute | solution.py:21
  422.1 8.2 %copy-start.7 = (bf16[4,4,128,128]{3,1,2,0:T(4,128)(2,1)S(1)}, bf16[4,4,128,128]{3,1,2,0:T(4,128)(2,1)}, u32[]{:S(2)}) copy-start(bf16[4,4,128,128]{3,1,2,0:T(4,128)(2,1)} %copy-done.6) | copy-start | bytes 1572868
  422.1 6.2 collective-permute-start.11
  440.7 3.1 copy-start.12
  636.6 3.5 copy-start.1
where the time goes:
time: 647 us; the launch traced here: 641 us
  waiting for transfers between devices  290 us (45%)
  local copies, waits for them, and re-layouts  162 us (25%)
  matrix products  76.5 us (12%)
  loops' own time  38 us (6%)
  other arithmetic  35 us (5%)
  starting transfers between devices  28.1 us (4%)
  blocking collectives  8.91 us (1%)
    ppermute x12, waiting for transfers between devices, swapped(): return lax.ppermute(block, axis, route)  163 us
    all_to_all x1, waiting for transfers between devices, on_device(): lax.all_to_all(outgoing.reshape(tile_count, SLOT_CAP, band_count, patch_s...  127 us
    dynamic_update_slice x16, local copies, waits for them, and re-layouts, place(): return lax.dynamic_update_slice(canvas, region + patch_model, anchor)  122 us
    another operation x1, loops' own time, on_device(): canvas = lax.fori_loop(0, piece_count, place, canvas_start)  38 us
    add x16, other arithmetic, place(): return lax.dynamic_update_slice(canvas, region + patch_model, anchor)  22 us
    dot_general x5, matrix products, refine(): jnp.einsum('nkij,nbij->nkb', morph, grad, precision=lax.Precision.HIGHEST)  19.5 us
    dot_general x6, matrix products, refine(): jnp.einsum('nkb,nbij->nkij', sed, grad, precision=lax.Precision.HIGHEST)  16.1 us
    all_to_all x1, starting transfers between devices, on_device(): lax.all_to_all(back_model.reshape(tile_count, SLOT_CAP, band_count, patch...  15 us
  transfers between devices with their start and end apart: 14, of which 13 were waited for; matrix products, arithmetic and copies ran while one was open for 2% of the time, Pallas kernels for 0%

commit v1 on v0

v1 whole, which is shorter than its diff:
```python
import functools

import jax
import jax.numpy as jnp
from jax import lax
from jax.experimental import pallas as pl
from jax.experimental.pallas import tpu as pltpu
from jax.sharding import PartitionSpec as P

TILE = 256
ITERS = 3
GROUP = 8
MESH = pl.DeviceIdType.MESH
F32 = jnp.float32
BF16 = jnp.bfloat16

step_size = 0.1

VMEM = pl.BlockSpec(memory_space=pltpu.VMEM)
SMEM = pl.BlockSpec(memory_space=pltpu.SMEM)
ANY = pl.BlockSpec(memory_space=pl.ANY)


def matmul(a, b):
    return jnp.dot(a, b, preferred_element_type=F32)


def matmul_t(a, b):
    return lax.dot_general(a, b, (((1,), (1,)), ((), ())), preferred_element_type=F32)


def t_matmul(a, b):
    return lax.dot_general(a, b, (((0,), (0,)), ((), ())), preferred_element_type=F32)


def barrier_all(me, count):
    barrier = pltpu.get_barrier_semaphore()
    for k in range(1, count):
        pl.semaphore_signal(
            barrier, inc=1, device_id={"tiles": lax.rem(me + k, count)}, device_id_type=MESH
        )
    pl.semaphore_wait(barrier, count - 1)


def remote(src, dst, send_sem, recv_sem, peer):
    return pltpu.make_async_remote_copy(
        src_ref=src,
        dst_ref=dst,
        send_sem=send_sem,
        recv_sem=recv_sem,
        device_id={"tiles": peer},
        device_id_type=MESH,
    )


def mix_band(sed_ref, morph_ref, b, bands, sources):
    total = sed_ref[b : b + 1, :] * morph_ref[0]
    for k in range(1, sources):
        row = k * bands + b
        total = total + sed_ref[row : row + 1, :] * morph_ref[k]
    return total.astype(BF16)


def blur_band(mix, kernel):
    return matmul_t(matmul(kernel, mix).astype(BF16), kernel)


def adjoint_band(resid, kernel):
    return matmul(t_matmul(kernel, resid).astype(BF16), kernel)


def update(sed_ref, morph_ref, grad_ref, part_ref, energy_ref, act_rows, bands, sources):
    for k in range(sources):
        morph = morph_ref[k]
        energy = jnp.sum(morph * morph, axis=0, keepdims=True)
        push = None
        for b in range(bands):
            row = k * bands + b
            grad = grad_ref[b]
            part_ref[row : row + 1, :] = jnp.sum(morph * grad, axis=0, keepdims=True)
            energy_ref[row : row + 1, :] = energy
            term = sed_ref[row : row + 1, :] * grad
            push = term if push is None else push + term
        fresh = jnp.maximum(morph + step_size * push, 0.0)
        if act_rows is not None:
            fresh = fresh * act_rows[k * bands : k * bands + 1, :]
        morph_ref[k] = fresh
    inner = jnp.sum(part_ref[...], axis=1, keepdims=True)
    energy = jnp.sum(energy_ref[...], axis=1, keepdims=True)
    sed = jnp.maximum(sed_ref[...] + inner / (energy + 1.0), 0.0)
    if act_rows is not None:
        sed = sed * act_rows[...]
    sed_ref[...] = sed


def first_kernel(
    count,
    bands,
    sources,
    pieces_ref,
    giant_ref,
    labels_ref,
    spectra_ref,
    psf_ref,
    recv_ref,
    morph_ref,
    scatter_buf,
    base_buf,
    resid_buf,
    blurred,
    image_part,
    sed_ref,
    grad_ref,
    part_ref,
    energy_ref,
    own_sem,
    send_sem,
    recv_sem,
    rs_send,
    rs_recv,
    ag_send,
    ag_recv,
):
    me = lax.axis_index("tiles")
    rank = lax.rem(me, GROUP)
    base = me - rank
    barrier_all(me, count)

    def scatter_copies(slot, src):
        copies = []
        for k in range(1, GROUP):
            other = lax.rem(rank + k, GROUP)
            copies.append(
                remote(
                    src.at[:, other],
                    scatter_buf.at[slot, rank],
                    rs_send.at[slot, k - 1],
                    rs_recv.at[slot, k - 1],
                    base + other,
                )
            )
        return copies

    def gather_copies(slot, ref):
        copies = []
        for k in range(1, GROUP):
            other = lax.rem(rank + k, GROUP)
            copies.append(
                remote(
                    ref.at[rank],
                    ref.at[rank],
                    ag_send.at[slot, k - 1],
                    ag_recv.at[slot, k - 1],
                    base + other,
                )
            )
        return copies

    def others_sum(slot, own):
        total = own.astype(F32)
        for k in range(1, GROUP):
            source = lax.rem(rank + GROUP - k, GROUP)
            total = total + scatter_buf[slot, source].astype(F32)
        return total

    opening = scatter_copies(ITERS, giant_ref)
    for copy in opening:
        copy.start()
    own = pltpu.make_async_copy(pieces_ref.at[:, me], recv_ref.at[me], own_sem)
    own.start()
    exchange = []
    for k in range(1, count):
        peer = lax.rem(me + k, count)
        copy = remote(
            pieces_ref.at[:, peer], recv_ref.at[me], send_sem.at[k - 1], recv_sem.at[k - 1], peer
        )
        copy.start()
        exchange.append(copy)

    for copy in opening:
        copy.wait_recv()
    image = others_sum(ITERS, giant_ref[:, rank])
    image_part[...] = image
    mean = image[0]
    for b in range(1, bands):
        mean = mean + image[b]
    base_buf[rank] = jnp.maximum(mean / bands, 0.0)
    spread = gather_copies(ITERS, base_buf)
    for copy in spread:
        copy.start()
    sed_ref[...] = spectra_ref[...]
    for copy in spread:
        copy.wait()
    for copy in opening:
        copy.wait_send()
    side = labels_ref.shape[0]
    base_map = base_buf[...].reshape(side, side)
    for k in range(sources):
        morph_ref[k] = jnp.where(labels_ref[...] == k + 1, base_map, 0.0)

    def iteration(it, carry):
        for b in range(bands):
            mix = mix_band(sed_ref, morph_ref, b, bands, sources)
            blurred[it, b] = (
                blur_band(mix, psf_ref[b]).astype(BF16).reshape(GROUP, side // GROUP, side)
            )
        sends = scatter_copies(it, blurred.at[it])
        for copy in sends:
            copy.start()
        for copy in sends:
            copy.wait()
        model = others_sum(it, blurred[it, :, rank])
        resid_buf[it, rank] = (image_part[...] - model).astype(BF16)
        shares = gather_copies(it, resid_buf.at[it])
        for copy in shares:
            copy.start()
        for copy in shares:
            copy.wait()
        for b in range(bands):
            resid = resid_buf[it, :, b].reshape(side, side)
            grad_ref[b] = adjoint_band(resid, psf_ref[b])
        update(sed_ref, morph_ref, grad_ref, part_ref, energy_ref, None, bands, sources)
        return carry

    lax.fori_loop(0, ITERS, iteration, 0)
    own.wait()
    for copy in exchange:
        copy.wait()


def segment_kernel(homes_ref, recv_ref, out_ref, total):
    total[...] = jnp.zeros_like(total)

    def add(index, carry):
        home = homes_ref[index]
        total[home] = total[home] + recv_ref[index].astype(F32)
        return carry

    lax.fori_loop(0, recv_ref.shape[0], add, 0, unroll=4)
    out_ref[...] = total[...].astype(BF16)


def owner_kernel(count, owned, src_ref, dst_ref, own_sem, send_sem, recv_sem):
    me = lax.axis_index("tiles")
    barrier_all(me, count)
    own = pltpu.make_async_copy(
        src_ref.at[pl.ds(me * owned, owned)], dst_ref.at[:, me], own_sem
    )
    own.start()
    copies = []
    for k in range(1, count):
        peer = lax.rem(me + k, count)
        copy = remote(
            src_ref.at[pl.ds(peer * owned, owned)],
            dst_ref.at[:, me],
            send_sem.at[k - 1],
            recv_sem.at[k - 1],
            peer,
        )
        copy.start()
        copies.append(copy)
    own.wait()
    for copy in copies:
        copy.wait()


def blend_kernel(
    bands,
    sources,
    image_ref,
    labels_ref,
    spectra_ref,
    active_ref,
    psf_ref,
    out_morph,
    out_sed,
    out_model,
    morph_ref,
    sed_ref,
    grad_ref,
    part_ref,
    energy_ref,
):
    act = active_ref.at[0]
    sed_ref[...] = spectra_ref[0] * active_ref[0]
    mean = image_ref[0, 0].astype(F32)
    for b in range(1, bands):
        mean = mean + image_ref[0, b].astype(F32)
    base_map = jnp.maximum(mean / bands, 0.0)
    for k in range(sources):
        morph_ref[k] = (
            jnp.where(labels_ref[0] == k + 1, base_map, 0.0) * act[k * bands : k * bands + 1, :]
        )

    def iteration(it, carry):
        for b in range(bands):
            kernel = psf_ref[b]
            mix = mix_band(sed_ref, morph_ref, b, bands, sources)
            resid = (image_ref[0, b].astype(F32) - blur_band(mix, kernel)).astype(BF16)
            grad_ref[b] = adjoint_band(resid, kernel)
        update(sed_ref, morph_ref, grad_ref, part_ref, energy_ref, act, bands, sources)
        return carry

    lax.fori_loop(0, ITERS, iteration, 0)
    out_morph[0] = morph_ref[...].astype(BF16)
    morph_ref[...] = morph_ref[...].astype(BF16).astype(F32)
    sed_ref[...] = sed_ref[...].astype(BF16).astype(F32)
    out_sed[0] = sed_ref[...]
    for b in range(bands):
        mix = mix_band(sed_ref, morph_ref, b, bands, sources)
        out_model[0, b] = blur_band(mix, psf_ref[b]).astype(BF16)


def return_kernel(
    count,
    owned,
    piece_count,
    homes_ref,
    model_ref,
    out_ref,
    held,
    picked,
    own_sems,
    send_sem,
    recv_sem,
    send_two,
    recv_two,
):
    me = lax.axis_index("tiles")
    barrier_all(me, count)
    own = pltpu.make_async_copy(
        model_ref.at[:, me], held.at[pl.ds(me * owned, owned)], own_sems.at[0]
    )
    own.start()
    copies = []
    for k in range(1, count):
        peer = lax.rem(me + k, count)
        copy = remote(
            model_ref.at[:, peer],
            held.at[pl.ds(me * owned, owned)],
            send_sem.at[k - 1],
            recv_sem.at[k - 1],
            peer,
        )
        copy.start()
        copies.append(copy)
    own.wait()
    for copy in copies:
        copy.wait()

    def pick(target):
        def one(index, carry):
            picked[target, index] = held[homes_ref[target * piece_count + index]]
            return carry

        lax.fori_loop(0, piece_count, one, 0)

    answers = []
    for k in range(1, count):
        peer = lax.rem(me + k, count)
        pick(peer)
        copy = remote(
            picked.at[peer], out_ref.at[:, me], send_two.at[k - 1], recv_two.at[k - 1], peer
        )
        copy.start()
        answers.append(copy)
    pick(me)
    last = pltpu.make_async_copy(picked.at[me], out_ref.at[:, me], own_sems.at[1])
    last.start()
    last.wait()
    for copy in answers:
        copy.wait()


def place_kernel(side, corners_ref, model_ref, out_ref, row_hot, col_hot):
    piece_count = model_ref.shape[0]

    @pl.when(pl.program_id(0) == 0)
    def _():
        rows = lax.broadcasted_iota(jnp.int32, (TILE, side), 0)
        inner = lax.broadcasted_iota(jnp.int32, (TILE, side), 1)
        inner_c = lax.broadcasted_iota(jnp.int32, (side, TILE), 0)
        cols = lax.broadcasted_iota(jnp.int32, (side, TILE), 1)

        def build(index, carry):
            row_hot[index] = jnp.where(rows == inner + corners_ref[index, 0], 1.0, 0.0).astype(BF16)
            col_hot[index] = jnp.where(cols == inner_c + corners_ref[index, 1], 1.0, 0.0).astype(
                BF16
            )
            return carry

        lax.fori_loop(0, piece_count, build, 0)

    total = jnp.zeros((TILE, TILE), F32)
    for index in range(piece_count):
        wide = matmul(model_ref[index, 0], col_hot[index]).astype(BF16)
        total = total + matmul(row_hot[index], wide)
    out_ref[0] = total


def on_device(
    pieces,
    piece_blend,
    corners,
    blend_home,
    source_count,
    footprint,
    spectra,
    giant_pieces,
    giant_footprint,
    giant_spectra,
    psf_matrix,
):
    count = lax.axis_size("tiles")
    piece_count, bands, side, _ = pieces.shape
    owned = footprint.shape[0]
    blend_count = blend_home.shape[0]
    sources = spectra.shape[1]
    rows = bands * side // count
    lanes = side
    table = sources * bands
    lookup = piece_blend[:, None] == jnp.arange(blend_count, dtype=jnp.int32)[None, :]
    piece_home = jnp.sum(jnp.where(lookup, blend_home[None, :], 0), axis=1)
    homes = lax.all_gather(piece_home, "tiles", axis=0, tiled=True)

    dma = pltpu.SemaphoreType.DMA
    strip = side // GROUP
    recv, giant_morph = pl.pallas_call(
        functools.partial(first_kernel, count, bands, sources),
        out_shape=(
            jax.ShapeDtypeStruct((count, piece_count, rows, lanes), BF16),
            jax.ShapeDtypeStruct((sources, side, side), F32),
        ),
        in_specs=[ANY, VMEM, VMEM, VMEM, VMEM],
        out_specs=(ANY, VMEM),
        scratch_shapes=[
            pltpu.VMEM((ITERS + 1, GROUP, bands, strip, side), BF16),
            pltpu.VMEM((GROUP, strip, side), F32),
            pltpu.VMEM((ITERS, GROUP, bands, strip, side), BF16),
            pltpu.VMEM((ITERS, bands, GROUP, strip, side), BF16),
            pltpu.VMEM((bands, strip, side), F32),
            pltpu.VMEM((table, lanes), F32),
            pltpu.VMEM((bands, side, side), F32),
            pltpu.VMEM((table, lanes), F32),
            pltpu.VMEM((table, lanes), F32),
            dma,
            dma((count - 1,)),
            dma((count - 1,)),
            dma((ITERS + 1, GROUP - 1)),
            dma((ITERS + 1, GROUP - 1)),
            dma((ITERS + 1, GROUP - 1)),
            dma((ITERS + 1, GROUP - 1)),
        ],
        compiler_params=pltpu.CompilerParams(collective_id=0, has_side_effects=True),
        name="first",
    )(
        pieces.reshape(piece_count, count, rows, lanes),
        giant_pieces.reshape(bands, GROUP, strip, side),
        giant_footprint[0],
        jnp.broadcast_to(giant_spectra.reshape(table, 1), (table, lanes)),
        psf_matrix,
    )

    summed = pl.pallas_call(
        segment_kernel,
        out_shape=jax.ShapeDtypeStruct((blend_count, rows, lanes), BF16),
        in_specs=[SMEM, VMEM],
        out_specs=VMEM,
        scratch_shapes=[pltpu.VMEM((blend_count, rows, lanes), F32)],
        name="segment",
    )(homes, recv.reshape(count * piece_count, rows, lanes))

    image = pl.pallas_call(
        functools.partial(owner_kernel, count, owned),
        out_shape=jax.ShapeDtypeStruct((owned, count, rows, lanes), BF16),
        in_specs=[VMEM],
        out_specs=VMEM,
        scratch_shapes=[dma, dma((count - 1,)), dma((count - 1,))],
        compiler_params=pltpu.CompilerParams(collective_id=1, has_side_effects=True),
        name="owner",
    )(summed)

    active = (jnp.arange(sources, dtype=jnp.int32)[None, :] < source_count[:, None]).astype(F32)
    active_rows = jnp.broadcast_to(
        jnp.repeat(active, bands, axis=1)[:, :, None], (owned, table, lanes)
    )
    spectra_rows = jnp.broadcast_to(spectra.reshape(owned, table, 1), (owned, table, lanes))
    final_morph, sed_rows, model = pl.pallas_call(
        functools.partial(blend_kernel, bands, sources),
        grid=(owned,),
        out_shape=(
            jax.ShapeDtypeStruct((owned, sources, side, side), BF16),
            jax.ShapeDtypeStruct((owned, table, lanes), F32),
            jax.ShapeDtypeStruct((owned, bands, side, side), BF16),
        ),
        in_specs=[
            pl.BlockSpec((1, bands, side, side), lambda n: (n, 0, 0, 0)),
            pl.BlockSpec((1, side, side), lambda n: (n, 0, 0)),
            pl.BlockSpec((1, table, lanes), lambda n: (n, 0, 0)),
            pl.BlockSpec((1, table, lanes), lambda n: (n, 0, 0)),
            pl.BlockSpec((bands, side, side), lambda n: (0, 0, 0)),
        ],
        out_specs=(
            pl.BlockSpec((1, sources, side, side), lambda n: (n, 0, 0, 0)),
            pl.BlockSpec((1, table, lanes), lambda n: (n, 0, 0)),
            pl.BlockSpec((1, bands, side, side), lambda n: (n, 0, 0, 0)),
        ),
        scratch_shapes=[
            pltpu.VMEM((sources, side, side), F32),
            pltpu.VMEM((table, lanes), F32),
            pltpu.VMEM((bands, side, side), F32),
            pltpu.VMEM((table, lanes), F32),
            pltpu.VMEM((table, lanes), F32),
        ],
        name="blend",
    )(
        image.reshape(owned, bands, side, side),
        footprint,
        spectra_rows,
        active_rows,
        psf_matrix,
    )
    final_sed = sed_rows[:, :, 0].reshape(owned, sources, bands).astype(BF16)

    piece_model = pl.pallas_call(
        functools.partial(return_kernel, count, owned, piece_count),
        out_shape=jax.ShapeDtypeStruct((piece_count, count, rows, lanes), BF16),
        in_specs=[SMEM, VMEM],
        out_specs=VMEM,
        scratch_shapes=[
            pltpu.VMEM((blend_count, rows, lanes), BF16),
            pltpu.VMEM((count, piece_count, rows, lanes), BF16),
            dma((2,)),
            dma((count - 1,)),
            dma((count - 1,)),
            dma((count - 1,)),
            dma((count - 1,)),
        ],
        compiler_params=pltpu.CompilerParams(collective_id=2, has_side_effects=True),
        name="back",
    )(homes, model.reshape(owned, count, rows, lanes))

    tile_model = pl.pallas_call(
        functools.partial(place_kernel, side),
        grid=(bands,),
        out_shape=jax.ShapeDtypeStruct((bands, TILE, TILE), F32),
        in_specs=[SMEM, pl.BlockSpec((piece_count, 1, side, side), lambda b: (0, b, 0, 0))],
        out_specs=pl.BlockSpec((1, TILE, TILE), lambda b: (b, 0, 0)),
        scratch_shapes=[
            pltpu.VMEM((piece_count, TILE, side), BF16),
            pltpu.VMEM((piece_count, side, TILE), BF16),
        ],
        name="place",
    )(corners, piece_model.reshape(piece_count, bands, side, side))
    return (final_morph, final_sed, tile_model[None], giant_morph[None])


def solution(mesh):
    in_specs = (
        P(("groups", "tiles"), None, None, None),
        P(("groups", "tiles")),
        P(("groups", "tiles"), None),
        P("groups"),
        P(("groups", "tiles")),
        P(("groups", "tiles"), None, None),
        P(("groups", "tiles"), None, None),
        P(("groups", "tiles"), None, None, None),
        P(("groups", "tiles"), None, None),
        P(("groups", "tiles"), None, None),
        P(),
    )
    out_specs = (
        P(("groups", "tiles"), None, None, None),
        P(("groups", "tiles"), None, None),
        P(("groups", "tiles"), None, None, None),
        P(("groups", "tiles"), None, None, None),
    )
    return jax.shard_map(
        on_device, mesh=mesh, in_specs=in_specs, out_specs=out_specs, check_vma=False
    )
```

time: 647 us -> 290 us (0.45)
  the two profiles are of different devices: /device:TPU:26 before, /device:TPU:15 now
where the time goes in v1:
time: 290 us; the launch traced here: 289 us
  Pallas kernels  269 us (93%)
  local copies, waits for them, and re-layouts  8.82 us (3%)
  blocking collectives  8.47 us (3%)
    pallas_call x1, Pallas kernels, on_device(): pl.pallas_call(functools.partial(first_kernel, count, bands, sources), ou...  99.5 us
    pallas_call x1, Pallas kernels, on_device(): pl.pallas_call(functools.partial(return_kernel, count, owned, piece_count...  93.6 us
    pallas_call x1, Pallas kernels, on_device(): pl.pallas_call(functools.partial(blend_kernel, bands, sources), grid=(own...  30.6 us
    pallas_call x1, Pallas kernels, on_device(): pl.pallas_call(functools.partial(owner_kernel, count, owned), out_shape=j...  27.6 us
    pallas_call x1, Pallas kernels, on_device(): pl.pallas_call(functools.partial(place_kernel, side), grid=(bands,), out_...  13.6 us
    unnamed x1, blocking collectives  8.47 us

profile of v1, /device:TPU:15, one launch (start us, length us, event | category | flops | bytes accessed | tf_op | source)
XLA Modules:
  0.0 289.2 jit_solution(4557988656732640823)
XLA Ops:
  0.6 1.2 dynamic-slice
  2.5 0.9 select_reduce_fusion
  3.4 0.8 broadcast_in_dim.49
  4.2 0.2 dynamic-update-slice
  4.3 8.5 %all-reduce.homes_ref = s32[256]{0:T(256)} all-reduce(s32[256]{0:T(256)S(1)} %dynamic-update-slice), channel_id=1, replica_groups=mesh['groups'=2,'tiles'=16] {'tiles'}, use_global_device_ids=true, to_apply=%add | all-reduce | flops 256 | bytes 2048
  12.8 0.7 fusion.1
  13.5 0.8 broadcast_in_dim.51
  14.3 0.1 broadcast_in_dim.53
  14.4 0.1 broadcast_in_dim.54
  14.5 1.3 copy.17.corners_ref
  15.8 0.7 broadcast_in_dim.50.spectra_ref
  16.5 0.7 broadcast_in_dim.55.active_ref
  17.2 0.7 broadcast_in_dim.52.spectra_ref
  17.9 99.5 %first.1 = (bf16[16,16,48,128]{3,2,1,0:T(8,128)(2,1)}, f32[4,128,128]{2,1,0:T(8,128)}) custom-call(bf16[16,16,48,128]{3,2,1,0:T(8,128)(2,1)} %bitcast.11, bf16[6,8,16,128]{3,2,1,0:T(8,128)(2,1)} %bitcast.17, s32[128,128]{1,0:T(8,128)} %bitcast.18, f32[24,128]{1,0:T(8,128)} %broadcast_in_dim.50.spectra_ref, bf16[6,128,128]{2,1,0:T(8,128)(2,1)} %psf_ref.3), custom_call_target="tpu_custom_call" | custom-call | tf_op jit(solution)/shard_map/first/pallas_call | solution.py:428
  117.4 4.1 %segment.1.src_ref = bf16[64,48,128]{2,1,0:T(8,128)(2,1)} custom-call(s32[256]{0:T(256)} %all-reduce.homes_ref, bf16[256,48,128]{2,1,0:T(8,128)(2,1)} %bitcast.12), custom_call_target="tpu_custom_call" | custom-call | tf_op jit(solution)/shard_map/segment/pallas_call | solution.py:464
  121.5 27.6 %owner.1 = bf16[4,16,48,128]{3,2,1,0:T(8,128)(2,1)} custom-call(bf16[64,48,128]{2,1,0:T(8,128)(2,1)} %segment.1.src_ref), custom_call_target="tpu_custom_call" | custom-call | tf_op jit(solution)/shard_map/owner/pallas_call | solution.py:473
  149.1 30.6 %blend.1 = (bf16[4,4,128,128]{3,2,1,0:T(8,128)(2,1)}, f32[4,24,128]{2,1,0:T(8,128)}, bf16[4,6,128,128]{3,2,1,0:T(8,128)(2,1)}) custom-call(bf16[4,6,128,128]{3,2,1,0:T(8,128)(2,1)} %bitcast.13, s32[4,128,128]{2,1,0:T(8,128)} %labels_ref.1, f32[4,24,128]{2,1,0:T(8,128)} %broadcast_in_dim.52.spectra_ref, f32[4,24,128]{2,1,0:T(8,128)} %broadcast_in_dim.55.active_ref, ...), custom_call_target="tpu_custom_call" | custom-call | tf_op jit(solution)/shard_map/blend/pallas_call | solution.py:488
  179.8 0.9 fusion
  180.7 0.7 convert_element_type.8
  181.4 93.6 %back.1 = bf16[16,16,48,128]{3,2,1,0:T(8,128)(2,1)} custom-call(s32[256]{0:T(256)} %all-reduce.homes_ref, bf16[4,16,48,128]{3,2,1,0:T(8,128)(2,1)} %bitcast.15), custom_call_target="tpu_custom_call" | custom-call | tf_op jit(solution)/shard_map/back/pallas_call | solution.py:525
  274.9 0.0 copy-start
  274.9 13.6 %place.1 = f32[6,256,256]{2,1,0:T(8,128)} custom-call(s32[16,2]{1,0:T(8,128)} %copy.17.corners_ref, bf16[16,6,128,128]{3,2,1,0:T(8,128)(2,1)} %bitcast.10), custom_call_target="tpu_custom_call" | custom-call | tf_op jit(solution)/shard_map/place/pallas_call | solution.py:543
  288.5 0.0 copy-done
  288.5 0.7 copy.20
  (1 shorter events, 0.0 us)
Async XLA Ops:
  274.9 13.6 %copy-start = (f32[4,128,128]{2,1,0:T(8,128)S(1)}, f32[4,128,128]{2,1,0:T(8,128)}, u32[]{:S(2)}) copy-start(f32[4,128,128]{2,1,0:T(8,128)} %get-tuple-element.13) | copy-start | bytes 786436

commit v2 on v1

--- a/solution.py
+++ b/solution.py
@@ -98,12 +98,14 @@
     bands,
     sources,
     pieces_ref,
+    home_ref,
     giant_ref,
     labels_ref,
     spectra_ref,
     psf_ref,
     recv_ref,
     morph_ref,
+    homes_ref,
     scatter_buf,
     base_buf,
     resid_buf,
@@ -120,11 +122,21 @@
     rs_recv,
     ag_send,
     ag_recv,
+    home_send,
+    home_recv,
 ):
     me = lax.axis_index("tiles")
     rank = lax.rem(me, GROUP)
     base = me - rank
-    barrier_all(me, count)
+    barrier = pltpu.get_barrier_semaphore()
+    for k in range(1, GROUP):
+        pl.semaphore_signal(
+            barrier,
+            inc=1,
+            device_id={"tiles": base + lax.rem(rank + k, GROUP)},
+            device_id_type=MESH,
+        )
+    pl.semaphore_wait(barrier, GROUP - 1)
 
     def scatter_copies(slot, src):
         copies = []
@@ -166,16 +178,34 @@
     opening = scatter_copies(ITERS, giant_ref)
     for copy in opening:
         copy.start()
-    own = pltpu.make_async_copy(pieces_ref.at[:, me], recv_ref.at[me], own_sem)
+    homes_ref[rank] = home_ref[...]
+    exchange = []
+    for k in range(1, GROUP):
+        other = lax.rem(rank + k, GROUP)
+        exchange.append(
+            remote(
+                home_ref,
+                homes_ref.at[rank],
+                home_send.at[k - 1],
+                home_recv.at[k - 1],
+                base + other,
+            )
+        )
+    for k in range(1, GROUP):
+        other = lax.rem(rank + k, GROUP)
+        exchange.append(
+            remote(
+                pieces_ref.at[:, other],
+                recv_ref.at[rank],
+                send_sem.at[k - 1],
+                recv_sem.at[k - 1],
+                base + other,
+            )
+        )
+    for copy in exchange:
+        copy.start()
+    own = pltpu.make_async_copy(pieces_ref.at[:, rank], recv_ref.at[rank], own_sem)
     own.start()
-    exchange = []
-    for k in range(1, count):
-        peer = lax.rem(me + k, count)
-        copy = remote(
-            pieces_ref.at[:, peer], recv_ref.at[me], send_sem.at[k - 1], recv_sem.at[k - 1], peer
-        )
-        copy.start()
-        exchange.append(copy)
 
     for copy in opening:
         copy.wait_recv()
@@ -240,132 +270,150 @@
     out_ref[...] = total[...].astype(BF16)
 
 
-def owner_kernel(count, owned, src_ref, dst_ref, own_sem, send_sem, recv_sem):
-    me = lax.axis_index("tiles")
-    barrier_all(me, count)
-    own = pltpu.make_async_copy(
-        src_ref.at[pl.ds(me * owned, owned)], dst_ref.at[:, me], own_sem
-    )
-    own.start()
-    copies = []
-    for k in range(1, count):
-        peer = lax.rem(me + k, count)
-        copy = remote(
-            src_ref.at[pl.ds(peer * owned, owned)],
-            dst_ref.at[:, me],
-            send_sem.at[k - 1],
-            recv_sem.at[k - 1],
-            peer,
-        )
-        copy.start()
-        copies.append(copy)
-    own.wait()
-    for copy in copies:
-        copy.wait()
-
-
-def blend_kernel(
+def core_kernel(
+    count,
     bands,
     sources,
-    image_ref,
+    owned,
+    piece_count,
+    homes_ref,
+    summed_ref,
     labels_ref,
     spectra_ref,
     active_ref,
     psf_ref,
     out_morph,
     out_sed,
-    out_model,
+    out_ref,
+    arrived,
+    image_ref,
     morph_ref,
     sed_ref,
     grad_ref,
     part_ref,
     energy_ref,
-):
-    act = active_ref.at[0]
-    sed_ref[...] = spectra_ref[0] * active_ref[0]
-    mean = image_ref[0, 0].astype(F32)
-    for b in range(1, bands):
-        mean = mean + image_ref[0, b].astype(F32)
-    base_map = jnp.maximum(mean / bands, 0.0)
-    for k in range(sources):
-        morph_ref[k] = (
-            jnp.where(labels_ref[0] == k + 1, base_map, 0.0) * act[k * bands : k * bands + 1, :]
-        )
-
-    def iteration(it, carry):
-        for b in range(bands):
-            kernel = psf_ref[b]
-            mix = mix_band(sed_ref, morph_ref, b, bands, sources)
-            resid = (image_ref[0, b].astype(F32) - blur_band(mix, kernel)).astype(BF16)
-            grad_ref[b] = adjoint_band(resid, kernel)
-        update(sed_ref, morph_ref, grad_ref, part_ref, energy_ref, act, bands, sources)
-        return carry
-
-    lax.fori_loop(0, ITERS, iteration, 0)
-    out_morph[0] = morph_ref[...].astype(BF16)
-    morph_ref[...] = morph_ref[...].astype(BF16).astype(F32)
-    sed_ref[...] = sed_ref[...].astype(BF16).astype(F32)
-    out_sed[0] = sed_ref[...]
-    for b in range(bands):
-        mix = mix_band(sed_ref, morph_ref, b, bands, sources)
-        out_model[0, b] = blur_band(mix, psf_ref[b]).astype(BF16)
-
-
-def return_kernel(
-    count,
-    owned,
-    piece_count,
-    homes_ref,
     model_ref,
-    out_ref,
     held,
     picked,
     own_sems,
-    send_sem,
-    recv_sem,
-    send_two,
-    recv_two,
+    in_send,
+    in_recv,
+    back_send,
+    back_recv,
+    last_send,
+    last_recv,
 ):
     me = lax.axis_index("tiles")
+    rank = lax.rem(me, GROUP)
+    base = me - rank
+    mine = me // GROUP
+    groups = count // GROUP
+    side = labels_ref.shape[1]
     barrier_all(me, count)
-    own = pltpu.make_async_copy(
-        model_ref.at[:, me], held.at[pl.ds(me * owned, owned)], own_sems.at[0]
-    )
-    own.start()
-    copies = []
-    for k in range(1, count):
+
+    def incoming(n, k):
         peer = lax.rem(me + k, count)
-        copy = remote(
-            model_ref.at[:, peer],
-            held.at[pl.ds(me * owned, owned)],
-            send_sem.at[k - 1],
-            recv_sem.at[k - 1],
+        return remote(
+            summed_ref.at[peer * owned + n],
+            arrived.at[n, mine, rank],
+            in_send.at[n, k - 1],
+            in_recv.at[n, k - 1],
             peer,
         )
-        copy.start()
-        copies.append(copy)
-    own.wait()
-    for copy in copies:
-        copy.wait()
+
+    def outgoing(n, k):
+        peer = lax.rem(me + k, count)
+        return remote(
+            model_ref.at[n, lax.rem(peer, GROUP)],
+            held.at[me * owned + n],
+            back_send.at[n, k - 1],
+            back_recv.at[n, k - 1],
+            peer,
+        )
+
+    def launch(n, carry):
+        for k in range(1, count):
+            incoming(n, k).start()
+        return carry
+
+    lax.fori_loop(0, owned, launch, 0)
+
+    def blend(n, carry):
+        arrived[n, mine, rank] = summed_ref[me * owned + n]
+        for k in range(1, count):
+            incoming(n, k).wait_recv()
+        total = arrived[n, 0].astype(F32)
+        for g in range(1, groups):
+            total = total + arrived[n, g].astype(F32)
+        image_ref[...] = total.reshape(bands, side, side)
+        act = active_ref.at[n]
+        sed_ref[...] = spectra_ref[n] * active_ref[n]
+        mean = image_ref[0]
+        for b in range(1, bands):
+            mean = mean + image_ref[b]
+        base_map = jnp.maximum(mean / bands, 0.0)
+        for k in range(sources):
+            morph_ref[k] = (
+                jnp.where(labels_ref[n] == k + 1, base_map, 0.0)
+                * act[k * bands : k * bands + 1, :]
+            )
+
+        def iteration(it, carry):
+            for b in range(bands):
+                kernel = psf_ref[b]
+                mix = mix_band(sed_ref, morph_ref, b, bands, sources)
+                resid = (image_ref[b] - blur_band(mix, kernel)).astype(BF16)
+                grad_ref[b] = adjoint_band(resid, kernel)
+            update(sed_ref, morph_ref, grad_ref, part_ref, energy_ref, act, bands, sources)
+            return carry
+
+        lax.fori_loop(0, ITERS, iteration, 0)
+        out_morph[n] = morph_ref[...].astype(BF16)
+        morph_ref[...] = morph_ref[...].astype(BF16).astype(F32)
+        sed_ref[...] = sed_ref[...].astype(BF16).astype(F32)
+        out_sed[n] = sed_ref[...]
+        for b in range(bands):
+            mix = mix_band(sed_ref, morph_ref, b, bands, sources)
+            grad_ref[b] = blur_band(mix, psf_ref[b])
+        model_ref[n] = grad_ref[...].reshape(model_ref.shape[1:]).astype(BF16)
+        held[me * owned + n] = model_ref[n, rank]
+        for k in range(1, count):
+            outgoing(n, k).start()
+        return carry
+
+    lax.fori_loop(0, owned, blend, 0)
+
+    def settle(n, carry):
+        for k in range(1, count):
+            incoming(n, k).wait_send()
+        for k in range(1, count):
+            outgoing(n, k).wait()
+        return carry
+
+    lax.fori_loop(0, owned, settle, 0)
 
     def pick(target):
         def one(index, carry):
             picked[target, index] = held[homes_ref[target * piece_count + index]]
             return carry
 
-        lax.fori_loop(0, piece_count, one, 0)
+        lax.fori_loop(0, piece_count, one, 0, unroll=4)
 
     answers = []
-    for k in range(1, count):
-        peer = lax.rem(me + k, count)
-        pick(peer)
+    for k in range(1, GROUP):
+        other = lax.rem(rank + k, GROUP)
+        pick(other)
         copy = remote(
-            picked.at[peer], out_ref.at[:, me], send_two.at[k - 1], recv_two.at[k - 1], peer
+            picked.at[other],
+            out_ref.at[:, rank],
+            last_send.at[k - 1],
+            last_recv.at[k - 1],
+            base + other,
         )
         copy.start()
         answers.append(copy)
-    pick(me)
-    last = pltpu.make_async_copy(picked.at[me], out_ref.at[:, me], own_sems.at[1])
+    pick(rank)
+    last = pltpu.make_async_copy(picked.at[rank], out_ref.at[:, rank], own_sems)
     last.start()
     last.wait()
     for copy in answers:
@@ -416,23 +464,25 @@
     owned = footprint.shape[0]
     blend_count = blend_home.shape[0]
     sources = spectra.shape[1]
-    rows = bands * side // count
+    rows = bands * side // GROUP
+    groups = count // GROUP
     lanes = side
     table = sources * bands
     lookup = piece_blend[:, None] == jnp.arange(blend_count, dtype=jnp.int32)[None, :]
     piece_home = jnp.sum(jnp.where(lookup, blend_home[None, :], 0), axis=1)
-    homes = lax.all_gather(piece_home, "tiles", axis=0, tiled=True)
+    home_rows = jnp.broadcast_to(jnp.pad(piece_home, (0, side - piece_count)), (8, side))
 
     dma = pltpu.SemaphoreType.DMA
     strip = side // GROUP
-    recv, giant_morph = pl.pallas_call(
+    recv, giant_morph, every_home = pl.pallas_call(
         functools.partial(first_kernel, count, bands, sources),
         out_shape=(
-            jax.ShapeDtypeStruct((count, piece_count, rows, lanes), BF16),
+            jax.ShapeDtypeStruct((GROUP, piece_count, rows, lanes), BF16),
             jax.ShapeDtypeStruct((sources, side, side), F32),
+            jax.ShapeDtypeStruct((GROUP, 8, side), jnp.int32),
         ),
-        in_specs=[ANY, VMEM, VMEM, VMEM, VMEM],
-        out_specs=(ANY, VMEM),
+        in_specs=[ANY, VMEM, VMEM, VMEM, VMEM, VMEM],
+        out_specs=(ANY, VMEM, VMEM),
         scratch_shapes=[
             pltpu.VMEM((ITERS + 1, GROUP, bands, strip, side), BF16),
             pltpu.VMEM((GROUP, strip, side), F32),
@@ -444,23 +494,27 @@
             pltpu.VMEM((table, lanes), F32),
             pltpu.VMEM((table, lanes), F32),
             dma,
-            dma((count - 1,)),
-            dma((count - 1,)),
+            dma((GROUP - 1,)),
+            dma((GROUP - 1,)),
             dma((ITERS + 1, GROUP - 1)),
             dma((ITERS + 1, GROUP - 1)),
             dma((ITERS + 1, GROUP - 1)),
             dma((ITERS + 1, GROUP - 1)),
+            dma((GROUP - 1,)),
+            dma((GROUP - 1,)),
         ],
         compiler_params=pltpu.CompilerParams(collective_id=0, has_side_effects=True),
         name="first",
     )(
-        pieces.reshape(piece_count, count, rows, lanes),
+        pieces.reshape(piece_count, GROUP, rows, lanes),
+        home_rows,
         giant_pieces.reshape(bands, GROUP, strip, side),
         giant_footprint[0],
         jnp.broadcast_to(giant_spectra.reshape(table, 1), (table, lanes)),
         psf_matrix,
     )
 
+    homes = every_home[:, 0, :piece_count].reshape(-1)
     summed = pl.pallas_call(
         segment_kernel,
         out_shape=jax.ShapeDtypeStruct((blend_count, rows, lanes), BF16),
@@ -468,77 +522,46 @@
         out_specs=VMEM,
         scratch_shapes=[pltpu.VMEM((blend_count, rows, lanes), F32)],
         name="segment",
-    )(homes, recv.reshape(count * piece_count, rows, lanes))
-
-    image = pl.pallas_call(
-        functools.partial(owner_kernel, count, owned),
-        out_shape=jax.ShapeDtypeStruct((owned, count, rows, lanes), BF16),
-        in_specs=[VMEM],
-        out_specs=VMEM,
-        scratch_shapes=[dma, dma((count - 1,)), dma((count - 1,))],
-        compiler_params=pltpu.CompilerParams(collective_id=1, has_side_effects=True),
-        name="owner",
-    )(summed)
+    )(homes, recv.reshape(GROUP * piece_count, rows, lanes))
 
     active = (jnp.arange(sources, dtype=jnp.int32)[None, :] < source_count[:, None]).astype(F32)
     active_rows = jnp.broadcast_to(
         jnp.repeat(active, bands, axis=1)[:, :, None], (owned, table, lanes)
     )
     spectra_rows = jnp.broadcast_to(spectra.reshape(owned, table, 1), (owned, table, lanes))
-    final_morph, sed_rows, model = pl.pallas_call(
-        functools.partial(blend_kernel, bands, sources),
-        grid=(owned,),
+    chunk = (GROUP, rows, lanes)
+    final_morph, sed_rows, piece_model = pl.pallas_call(
+        functools.partial(core_kernel, count, bands, sources, owned, piece_count),
         out_shape=(
             jax.ShapeDtypeStruct((owned, sources, side, side), BF16),
             jax.ShapeDtypeStruct((owned, table, lanes), F32),
-            jax.ShapeDtypeStruct((owned, bands, side, side), BF16),
+            jax.ShapeDtypeStruct((piece_count, GROUP, rows, lanes), BF16),
         ),
-        in_specs=[
-            pl.BlockSpec((1, bands, side, side), lambda n: (n, 0, 0, 0)),
-            pl.BlockSpec((1, side, side), lambda n: (n, 0, 0)),
-            pl.BlockSpec((1, table, lanes), lambda n: (n, 0, 0)),
-            pl.BlockSpec((1, table, lanes), lambda n: (n, 0, 0)),
-            pl.BlockSpec((bands, side, side), lambda n: (0, 0, 0)),
-        ],
-        out_specs=(
-            pl.BlockSpec((1, sources, side, side), lambda n: (n, 0, 0, 0)),
-            pl.BlockSpec((1, table, lanes), lambda n: (n, 0, 0)),
-            pl.BlockSpec((1, bands, side, side), lambda n: (n, 0, 0, 0)),
-        ),
+        in_specs=[SMEM, VMEM, VMEM, VMEM, VMEM, VMEM],
+        out_specs=(VMEM, VMEM, VMEM),
         scratch_shapes=[
+            pltpu.VMEM((owned, groups) + chunk, BF16),
+            pltpu.VMEM((bands, side, side), F32),
             pltpu.VMEM((sources, side, side), F32),
             pltpu.VMEM((table, lanes), F32),
             pltpu.VMEM((bands, side, side), F32),
             pltpu.VMEM((table, lanes), F32),
             pltpu.VMEM((table, lanes), F32),
+            pltpu.VMEM((owned,) + chunk, BF16),
+            pltpu.VMEM((blend_count, rows, lanes), BF16),
+            pltpu.VMEM((GROUP, piece_count, rows, lanes), BF16),
+            dma,
+            dma((owned, count - 1)),
+            dma((owned, count - 1)),
+            dma((owned, count - 1)),
+            dma((owned, count - 1)),
+            dma((GROUP - 1,)),
+            dma((GROUP - 1,)),
         ],
-        name="blend",
-    )(
-        image.reshape(owned, bands, side, side),
-        footprint,
-        spectra_rows,
-        active_rows,
-        psf_matrix,
-    )
+        compiler_params=pltpu.CompilerParams(collective_id=1, has_side_effects=True),
+        name="core",
+    )(homes, summed, footprint, spectra_rows, active_rows, psf_matrix)
     final_sed = sed_rows[:, :, 0].reshape(owned, sources, bands).astype(BF16)
-
-    piece_model = pl.pallas_call(
-        functools.partial(return_kernel, count, owned, piece_count),
-        out_shape=jax.ShapeDtypeStruct((piece_count, count, rows, lanes), BF16),
-        in_specs=[SMEM, VMEM],
-        out_specs=VMEM,
-        scratch_shapes=[
-            pltpu.VMEM((blend_count, rows, lanes), BF16),
-            pltpu.VMEM((count, piece_count, rows, lanes), BF16),
-            dma((2,)),
-            dma((count - 1,)),
-            dma((count - 1,)),
-            dma((count - 1,)),
-            dma((count - 1,)),
-        ],
-        compiler_params=pltpu.CompilerParams(collective_id=2, has_side_effects=True),
-        name="back",
-    )(homes, model.reshape(owned, count, rows, lanes))
 
     tile_model = pl.pallas_call(
         functools.partial(place_kernel, side),

time: 290 us -> 214 us (0.74)
  the two profiles are of different devices: /device:TPU:15 before, /device:TPU:26 now
where the time goes in v2:
time: 214 us; the launch traced here: 211 us
  Pallas kernels  201 us (94%)
  local copies, waits for them, and re-layouts  8.05 us (4%)
    pallas_call x1, Pallas kernels, on_device(): pl.pallas_call(functools.partial(core_kernel, count, bands, sources, owne...  112 us
    pallas_call x1, Pallas kernels, on_device(): pl.pallas_call(functools.partial(first_kernel, count, bands, sources), ou...  71.7 us
    pallas_call x1, Pallas kernels, on_device(): pl.pallas_call(functools.partial(place_kernel, side), grid=(bands,), out_...  13.5 us

profile of v2, /device:TPU:26, one launch (start us, length us, event | category | flops | bytes accessed | tf_op | source)
XLA Modules:
  0.0 211.0 jit_solution(16750888715499345691)
XLA Ops:
  0.6 0.8 broadcast_in_dim.53
  1.4 0.7 broadcast_in_dim.54.spectra_ref
  2.1 0.9 select_reduce_fusion
  2.9 0.6 broadcast_in_dim.52.home_ref
  3.5 71.7 %first.1 = (bf16[8,16,96,128]{3,2,1,0:T(8,128)(2,1)}, f32[4,128,128]{2,1,0:T(8,128)}, s32[8,8,128]{2,1,0:T(8,128)}) custom-call(bf16[16,8,96,128]{3,2,1,0:T(8,128)(2,1)} %bitcast.7, s32[8,128]{1,0:T(8,128)} %broadcast_in_dim.52.home_ref, bf16[6,8,16,128]{3,2,1,0:T(8,128)(2,1)} %bitcast.12, s32[128,128]{1,0:T(8,128)} %bitcast.13, ...), custom_call_target="tpu_custom_call" | custom-call | tf_op jit(solution)/shard_map/first/pallas_call | solution.py:477
  75.2 0.0 copy-start.5
  75.2 0.0 copy-start.3
  75.2 0.8 slice_reduce_fusion
  76.0 0.6 reshape_squeeze.4.homes_ref
  76.6 0.0 copy-start.4
  76.6 4.2 %segment.1.summed_ref = bf16[64,96,128]{2,1,0:T(8,128)(2,1)} custom-call(s32[128]{0:T(128)} %reshape_squeeze.4.homes_ref, bf16[128,96,128]{2,1,0:T(8,128)(2,1)} %bitcast.8), custom_call_target="tpu_custom_call" | custom-call | tf_op jit(solution)/shard_map/segment/pallas_call | solution.py:518
  80.9 0.0 copy-done.5
  80.9 0.1 fusion.1
  81.0 0.1 broadcast_in_dim.57
  81.0 0.1 broadcast_in_dim.58
  81.1 0.7 broadcast_in_dim.59.active_ref
  81.8 0.0 copy-done.3
  81.8 0.1 broadcast_in_dim.55
  81.9 0.7 broadcast_in_dim.56.spectra_ref
  82.6 111.8 %core.1 = (bf16[4,4,128,128]{3,2,1,0:T(8,128)(2,1)}, f32[4,24,128]{2,1,0:T(8,128)}, bf16[16,8,96,128]{3,2,1,0:T(8,128)(2,1)}) custom-call(s32[128]{0:T(128)} %reshape_squeeze.4.homes_ref, bf16[64,96,128]{2,1,0:T(8,128)(2,1)} %segment.1.summed_ref, s32[4,128,128]{2,1,0:T(8,128)} %labels_ref.1, f32[4,24,128]{2,1,0:T(8,128)} %broadcast_in_dim.56.spectra_ref, ...), custom_call_target="tpu_custom_call" | custom-call | tf_op jit(solution)/shard_map/core/pallas_call | solution.py:533
  194.4 0.0 copy-start.2
  194.5 0.0 copy-start
  194.5 0.0 copy-start.1
  194.5 0.0 copy-done.4
  194.5 0.7 copy.17.corners_ref
  195.2 13.5 %place.1 = f32[6,256,256]{2,1,0:T(8,128)} custom-call(s32[16,2]{1,0:T(8,128)} %copy.17.corners_ref, bf16[16,6,128,128]{3,2,1,0:T(8,128)(2,1)} %bitcast.9), custom_call_target="tpu_custom_call" | custom-call | tf_op jit(solution)/shard_map/place/pallas_call | solution.py:566
  208.7 0.0 copy-done.2
  208.7 0.1 fusion
  208.8 0.7 convert_element_type.8
  209.5 0.0 copy-done
  209.5 0.8 copy.20
  210.3 0.0 copy-done.1
  210.3 0.7 copy.21
  (1 shorter events, 0.0 us)
Async XLA Ops:
  75.2 5.7 %copy-start.5 = (s32[4]{0:T(128)S(1)}, s32[4]{0:T(128)}, u32[]{:S(2)}) copy-start(s32[4]{0:T(128)} %param.15) | copy-start | bytes 52
  75.2 6.6 %copy-start.3 = (f32[4,4,6]{2,1,0:T(4,128)S(1)}, f32[4,4,6]{2,1,0:T(4,128)}, u32[]{:S(2)}) copy-start(f32[4,4,6]{2,1,0:T(4,128)} %param.17) | copy-start | bytes 1156
  76.6 117.9 %copy-start.4 = (s32[16,2]{0,1:T(2,128)S(1)}, s32[16,2]{0,1:T(2,128)}, u32[]{:S(2)}) copy-start(s32[16,2]{0,1:T(2,128)} %param.13) | copy-start | bytes 388
  194.4 14.2 %copy-start.2 = (f32[4,24,128]{2,1,0:T(8,128)S(1)}, f32[4,24,128]{2,1,0:T(8,128)}, u32[]{:S(2)}) copy-start(f32[4,24,128]{2,1,0:T(8,128)} %get-tuple-element.13) | copy-start | bytes 147460
  194.5 15.0 %copy-start = (bf16[4,4,128,128]{3,2,1,0:T(8,128)(2,1)S(1)}, bf16[4,4,128,128]{3,2,1,0:T(8,128)(2,1)}, u32[]{:S(2)}) copy-start(bf16[4,4,128,128]{3,2,1,0:T(8,128)(2,1)} %get-tuple-element.20) | copy-start | bytes 1572868
  194.5 15.8 %copy-start.1 = (f32[4,128,128]{2,1,0:T(8,128)S(1)}, f32[4,128,128]{2,1,0:T(8,128)}, u32[]{:S(2)}) copy-start(f32[4,128,128]{2,1,0:T(8,128)} %get-tuple-element.15) | copy-start | bytes 786436

commit v3 on v2

--- a/solution.py
+++ b/solution.py
@@ -191,19 +191,22 @@
                 base + other,
             )
         )
-    for k in range(1, GROUP):
+    def piece_copy(k):
         other = lax.rem(rank + k, GROUP)
-        exchange.append(
-            remote(
-                pieces_ref.at[:, other],
-                recv_ref.at[rank],
-                send_sem.at[k - 1],
-                recv_sem.at[k - 1],
-                base + other,
-            )
+        return remote(
+            pieces_ref.at[:, other],
+            recv_ref.at[rank],
+            send_sem.at[k - 1],
+            recv_sem.at[k - 1],
+            base + other,
         )
+
     for copy in exchange:
         copy.start()
+    late = (GROUP - 1) // ITERS
+    early = GROUP - 1 - late * ITERS
+    for k in range(1, early + 1):
+        piece_copy(k).start()
     own = pltpu.make_async_copy(pieces_ref.at[:, rank], recv_ref.at[rank], own_sem)
     own.start()
 
@@ -229,6 +232,8 @@
         morph_ref[k] = jnp.where(labels_ref[...] == k + 1, base_map, 0.0)
 
     def iteration(it, carry):
+        for offset in range(late):
+            piece_copy(early + 1 + it * late + offset).start()
         for b in range(bands):
             mix = mix_band(sed_ref, morph_ref, b, bands, sources)
             blurred[it, b] = (
@@ -256,6 +261,8 @@
     own.wait()
     for copy in exchange:
         copy.wait()
+    for k in range(1, GROUP):
+        piece_copy(k).wait()
 
 
 def segment_kernel(homes_ref, recv_ref, out_ref, total):
@@ -420,7 +427,7 @@
         copy.wait()
 
 
-def place_kernel(side, corners_ref, model_ref, out_ref, row_hot, col_hot):
+def place_kernel(side, corners_ref, model_ref, out_ref, row_hot, col_hot, wide):
     piece_count = model_ref.shape[0]
 
     @pl.when(pl.program_id(0) == 0)
@@ -430,20 +437,19 @@
         inner_c = lax.broadcasted_iota(jnp.int32, (side, TILE), 0)
         cols = lax.broadcasted_iota(jnp.int32, (side, TILE), 1)
 
-        def build(index, carry):
-            row_hot[index] = jnp.where(rows == inner + corners_ref[index, 0], 1.0, 0.0).astype(BF16)
+        for index in range(piece_count):
+            row_hot[:, index * side : (index + 1) * side] = jnp.where(
+                rows == inner + corners_ref[index, 0], 1.0, 0.0
+            ).astype(BF16)
             col_hot[index] = jnp.where(cols == inner_c + corners_ref[index, 1], 1.0, 0.0).astype(
                 BF16
             )
-            return carry
-
-        lax.fori_loop(0, piece_count, build, 0)
-
-    total = jnp.zeros((TILE, TILE), F32)
+
     for index in range(piece_count):
-        wide = matmul(model_ref[index, 0], col_hot[index]).astype(BF16)
-        total = total + matmul(row_hot[index], wide)
-    out_ref[0] = total
+        wide[index * side : (index + 1) * side, :] = matmul(
+            model_ref[index, 0], col_hot[index]
+        ).astype(BF16)
+    out_ref[0] = matmul(row_hot[...], wide[...])
 
 
 def on_device(
@@ -570,8 +576,9 @@
         in_specs=[SMEM, pl.BlockSpec((piece_count, 1, side, side), lambda b: (0, b, 0, 0))],
         out_specs=pl.BlockSpec((1, TILE, TILE), lambda b: (b, 0, 0)),
         scratch_shapes=[
-            pltpu.VMEM((piece_count, TILE, side), BF16),
+            pltpu.VMEM((TILE, piece_count * side), BF16),
             pltpu.VMEM((piece_count, side, TILE), BF16),
+            pltpu.VMEM((piece_count * side, TILE), BF16),
         ],
         name="place",
     )(corners, piece_model.reshape(piece_count, bands, side, side))

time: 214 us -> 223 us (1.042)
  Pallas kernels: 201 us -> 211 us
    pallas_call x1, Pallas kernels: 71.7 us -> 87.3 us  [on_device(): pl.pallas_call(functools.partial(first_kernel, count, bands, sources), ou...]
    pallas_call x1, Pallas kernels: 13.5 us -> 7.6 us  [on_device(): pl.pallas_call(functools.partial(place_kernel, side), grid=(bands,), out_...]
where the time goes in v3:
time: 223 us; the launch traced here: 220 us
  Pallas kernels  211 us (95%)
  local copies, waits for them, and re-layouts  8.05 us (4%)
    pallas_call x1, Pallas kernels, on_device(): pl.pallas_call(functools.partial(core_kernel, count, bands, sources, owne...  112 us
    pallas_call x1, Pallas kernels, on_device(): pl.pallas_call(functools.partial(first_kernel, count, bands, sources), ou...  87.3 us
    pallas_call x1, Pallas kernels, on_device(): pl.pallas_call(functools.partial(place_kernel, side), grid=(bands,), out_...  7.6 us

profile of v3, /device:TPU:26, one launch (start us, length us, event | category | flops | bytes accessed | tf_op | source)
XLA Modules:
  0.0 220.5 jit_solution(2557189668647549739)
XLA Ops:
  0.6 0.8 broadcast_in_dim.53
  1.4 0.7 broadcast_in_dim.54.spectra_ref
  2.1 0.9 select_reduce_fusion
  2.9 0.6 broadcast_in_dim.52.home_ref
  3.5 87.3 %first.1 = (bf16[8,16,96,128]{3,2,1,0:T(8,128)(2,1)}, f32[4,128,128]{2,1,0:T(8,128)}, s32[8,8,128]{2,1,0:T(8,128)}) custom-call(bf16[16,8,96,128]{3,2,1,0:T(8,128)(2,1)} %bitcast.7, s32[8,128]{1,0:T(8,128)} %broadcast_in_dim.52.home_ref, bf16[6,8,16,128]{3,2,1,0:T(8,128)(2,1)} %bitcast.12, s32[128,128]{1,0:T(8,128)} %bitcast.13, ...), custom_call_target="tpu_custom_call" | custom-call | tf_op jit(solution)/shard_map/first/pallas_call | solution.py:483
  90.8 0.0 copy-start.5
  90.8 0.0 copy-start.3
  90.8 0.8 slice_reduce_fusion
  91.6 0.6 reshape_squeeze.4.homes_ref
  92.2 0.0 copy-start.4
  92.2 4.2 %segment.1.summed_ref = bf16[64,96,128]{2,1,0:T(8,128)(2,1)} custom-call(s32[128]{0:T(128)} %reshape_squeeze.4.homes_ref, bf16[128,96,128]{2,1,0:T(8,128)(2,1)} %bitcast.8), custom_call_target="tpu_custom_call" | custom-call | tf_op jit(solution)/shard_map/segment/pallas_call | solution.py:524
  96.4 0.0 copy-done.5
  96.4 0.1 fusion.1
  96.5 0.1 broadcast_in_dim.57
  96.6 0.1 broadcast_in_dim.58
  96.7 0.7 broadcast_in_dim.59.active_ref
  97.4 0.0 copy-done.3
  97.4 0.1 broadcast_in_dim.55
  97.5 0.7 broadcast_in_dim.56.spectra_ref
  98.2 111.7 %core.1 = (bf16[4,4,128,128]{3,2,1,0:T(8,128)(2,1)}, f32[4,24,128]{2,1,0:T(8,128)}, bf16[16,8,96,128]{3,2,1,0:T(8,128)(2,1)}) custom-call(s32[128]{0:T(128)} %reshape_squeeze.4.homes_ref, bf16[64,96,128]{2,1,0:T(8,128)(2,1)} %segment.1.summed_ref, s32[4,128,128]{2,1,0:T(8,128)} %labels_ref.1, f32[4,24,128]{2,1,0:T(8,128)} %broadcast_in_dim.56.spectra_ref, ...), custom_call_target="tpu_custom_call" | custom-call | tf_op jit(solution)/shard_map/core/pallas_call | solution.py:539
  209.8 0.0 copy-start.2
  209.9 0.0 copy-start
  209.9 0.0 copy-start.1
  209.9 0.0 copy-done.4
  209.9 0.7 copy.17.corners_ref
  210.6 7.6 %place.1 = f32[6,256,256]{2,1,0:T(8,128)} custom-call(s32[16,2]{1,0:T(8,128)} %copy.17.corners_ref, bf16[16,6,128,128]{3,2,1,0:T(8,128)(2,1)} %bitcast.9), custom_call_target="tpu_custom_call" | custom-call | tf_op jit(solution)/shard_map/place/pallas_call | solution.py:572
  218.2 0.0 copy-done.2
  218.2 0.1 fusion
  218.3 0.7 convert_element_type.8
  219.0 0.0 copy-done
  219.0 0.8 copy.20
  219.8 0.0 copy-done.1
  219.8 0.7 copy.21
  (1 shorter events, 0.0 us)
Async XLA Ops:
  90.8 5.7 %copy-start.5 = (s32[4]{0:T(128)S(1)}, s32[4]{0:T(128)}, u32[]{:S(2)}) copy-start(s32[4]{0:T(128)} %param.15) | copy-start | bytes 52
  90.8 6.6 %copy-start.3 = (f32[4,4,6]{2,1,0:T(4,128)S(1)}, f32[4,4,6]{2,1,0:T(4,128)}, u32[]{:S(2)}) copy-start(f32[4,4,6]{2,1,0:T(4,128)} %param.17) | copy-start | bytes 1156
  92.2 117.7 %copy-start.4 = (s32[16,2]{0,1:T(2,128)S(1)}, s32[16,2]{0,1:T(2,128)}, u32[]{:S(2)}) copy-start(s32[16,2]{0,1:T(2,128)} %param.13) | copy-start | bytes 388
  209.8 8.3 %copy-start.2 = (f32[4,24,128]{2,1,0:T(8,128)S(1)}, f32[4,24,128]{2,1,0:T(8,128)}, u32[]{:S(2)}) copy-start(f32[4,24,128]{2,1,0:T(8,128)} %get-tuple-element.13) | copy-start | bytes 147460
  209.9 9.1 %copy-start = (bf16[4,4,128,128]{3,2,1,0:T(8,128)(2,1)S(1)}, bf16[4,4,128,128]{3,2,1,0:T(8,128)(2,1)}, u32[]{:S(2)}) copy-start(bf16[4,4,128,128]{3,2,1,0:T(8,128)(2,1)} %get-tuple-element.20) | copy-start | bytes 1572868
  209.9 9.9 %copy-start.1 = (f32[4,128,128]{2,1,0:T(8,128)S(1)}, f32[4,128,128]{2,1,0:T(8,128)}, u32[]{:S(2)}) copy-start(f32[4,128,128]{2,1,0:T(8,128)} %get-tuple-element.15) | copy-start | bytes 786436
